TPU v7x, 32 devices: a whole 2x2x4 slice. The times are simulated.
32 devices in a mesh: guide: 2 (over core), blk: 16 (over z, y, x).
Axes of the slice: x: 2, y: 2, z: 4, core: 2. Of those that a mesh axis runs over, the one named last changes fastest.
Arguments:
- x_cols: bfloat16 [128, 2048], P(None, 'blk'), may hold values from -3 to 3
- queries: bfloat16 [128, 9216], P('blk'), may hold values from -64 to 64
- new_kv: bfloat16 [128, 576], P('blk'), may hold values from -6 to 6
- cache: bfloat16 [2, 128, 256, 576], P('guide', 'blk'), may hold values from -8 to 8
- lengths: int32 [2, 128], P('guide'), may hold values from 2 to 256, as said below
- perm: int32 [128], replicated, may hold values from 0 to 127, each once
- guide_scale: float32 [128], replicated, may hold values from 1.5 to 7.5
- w_uv: bfloat16 [16, 512, 128], replicated, may hold values from -0.75 to 0.75
- w_out: bfloat16 [2048, 2048], P(None, 'blk'), may hold values from -0.125 to 0.125
- mlp_gain: float32 [2048], replicated, may hold values from 0.5 to 1.5
- w_gate: bfloat16 [2048, 10944], P(None, 'blk'), may hold values from -0.125 to 0.125
- w_up: bfloat16 [2048, 10944], P(None, 'blk'), may hold values from -0.125 to 0.125
- w_down: bfloat16 [10944, 2048], P('blk'), may hold values from -0.0546875 to 0.0546875
- head_gain: float32 [2048], replicated, may hold values from 0.5 to 1.5
- w_head: bfloat16 [2048, 102400], P(None, 'blk'), may hold values from -0.125 to 0.125
Outputs:
- guided: bfloat16 [128, 102400], P('guide', 'blk')
Inputs may be any that keep to these rules, and one draw needn't show every extreme that they name: Positions 0 to lengths[g, r] - 1 of request r's cache in group g are live; each group has a request with 256 live positions. Slot s holds request perm[s]; every request has one slot.
All inputs are finite; a program needn't handle non-finite values.
Results may differ from a plain program's by a relative error of at most 0.018.
Values may be sent and summed in bfloat16 or wider, within the bound.
No kernel may reach another device: no remote copies, remote signals or barrier semaphores. Data moves between devices by JAX's collectives and lax.ppermute only.
A program may use at most 128 MiB of HBM per device.

v0:
```python
import jax
import jax.numpy as jnp
from jax import lax
from jax.sharding import PartitionSpec as P

FF = 10944


def partner(value, axis, apart):
    mask = 2**apart
    pairs = [(source, source ^ mask) for source in range(lax.axis_size(axis))]
    return lax.ppermute(value, axis, pairs)


def rms_round(hidden, gain):
    values = hidden.astype(jnp.float32)
    meansq = jnp.mean(values * values, axis=-1, keepdims=True)
    return (values * lax.rsqrt(meansq + 1e-06) * gain).astype(jnp.bfloat16)


def body(
    x_cols,
    queries,
    new_kv,
    cache,
    lengths,
    perm,
    guide_scale,
    w_uv,
    w_out,
    mlp_gain,
    w_gate,
    w_up,
    w_down,
    head_gain,
    w_head,
):
    guide_index = lax.axis_index("guide")
    blk_index = lax.axis_index("blk")
    slots_dev = queries.shape[0]
    heads_count = w_uv.shape[0]
    latent_size = w_uv.shape[1]
    key_width = new_kv.shape[1]
    score_scale = (w_uv.shape[2] + key_width - latent_size) ** (-0.5)
    slot_ids = blk_index * slots_dev + jnp.arange(slots_dev, dtype=jnp.int32)
    owners = jnp.take(perm, slot_ids)
    live_len = jnp.take(lengths[0], owners)
    query_heads = queries.reshape(slots_dev, heads_count, key_width)
    cached_keys = cache[0]
    scores = (
        jnp.einsum("shk,slk->shl", query_heads, cached_keys, preferred_element_type=jnp.float32)
        * score_scale
    )
    own_score = (
        jnp.einsum("shk,sk->sh", query_heads, new_kv, preferred_element_type=jnp.float32)
        * score_scale
    )
    live_mask = (
        jnp.arange(cached_keys.shape[1], dtype=jnp.int32)[None, None, :] < live_len[:, None, None]
    )
    scores = jnp.where(live_mask, scores, jnp.float32(-1e30))
    peak_score = jnp.maximum(jnp.max(scores, axis=-1), own_score)
    probs = jnp.where(live_mask, jnp.exp(scores - peak_score[..., None]), jnp.float32(0.0))
    own_prob = jnp.exp(own_score - peak_score)
    softmax_total = jnp.sum(probs, axis=-1) + own_prob
    weights = (probs / softmax_total[..., None]).astype(jnp.bfloat16)
    own_weight = (own_prob / softmax_total).astype(jnp.bfloat16)
    latent_out = jnp.einsum(
        "shl,slc->shc", weights, cached_keys[:, :, :latent_size], preferred_element_type=jnp.float32
    )
    latent_out = latent_out + own_weight.astype(jnp.float32)[..., None] * new_kv[
        :, None, :latent_size
    ].astype(jnp.float32)
    value_rows = jnp.einsum(
        "shc,hcd->shd", latent_out.astype(jnp.bfloat16), w_uv, preferred_element_type=jnp.float32
    )
    value_rows = value_rows.astype(jnp.bfloat16).reshape(slots_dev, -1)
    attended = jnp.dot(
        lax.all_gather(value_rows, "blk", axis=0, tiled=True),
        w_out,
        preferred_element_type=jnp.float32,
    )
    residual = (x_cols.astype(jnp.float32) + attended).astype(jnp.bfloat16)
    rows_full = lax.all_gather(residual, "blk", axis=1, tiled=True)
    normed = rms_round(rows_full, mlp_gain)
    unit_count = w_gate.shape[1]
    gate_out = jnp.dot(normed, w_gate, preferred_element_type=jnp.float32)
    up_out = jnp.dot(normed, w_up, preferred_element_type=jnp.float32)
    unit_ids = blk_index * unit_count + jnp.arange(unit_count, dtype=jnp.int32)
    hidden = jnp.where(
        unit_ids[None, :] < FF, jax.nn.silu(gate_out) * up_out, jnp.float32(0.0)
    ).astype(jnp.bfloat16)
    partial_sum = jnp.dot(hidden, w_down, preferred_element_type=jnp.float32)
    summed = lax.psum(partial_sum, "blk")
    after_mlp = (rows_full.astype(jnp.float32) + summed).astype(jnp.bfloat16)
    logits = jnp.dot(rms_round(after_mlp, head_gain), w_head, preferred_element_type=jnp.float32)
    request_count = logits.shape[0]
    half_rows = request_count // 2
    slot_scale = jnp.take(guide_scale, perm)
    request_order = (
        jnp.zeros((request_count,), jnp.int32)
        .at[perm]
        .set(jnp.arange(request_count, dtype=jnp.int32))
    )
    own_order = lax.dynamic_slice_in_dim(request_order, guide_index * half_rows, half_rows)
    other_logits = partner(logits.astype(jnp.bfloat16), "guide", 0).astype(logits.dtype)
    cond_logits = jnp.where(guide_index == 0, logits, other_logits)
    uncond_logits = jnp.where(guide_index == 0, other_logits, logits)
    mixed = (uncond_logits + slot_scale[:, None] * (cond_logits - uncond_logits)).astype(
        jnp.bfloat16
    )
    return jnp.take(mixed, own_order, axis=0)


def solution(mesh):
    return jax.shard_map(
        body,
        mesh=mesh,
        in_specs=(
            P(None, "blk"),
            P("blk", None),
            P("blk", None),
            P("guide", "blk", None, None),
            P("guide", None),
            P(),
            P(),
            P(),
            P(None, "blk"),
            P(),
            P(None, "blk"),
            P(None, "blk"),
            P("blk", None),
            P(),
            P(None, "blk"),
        ),
        out_specs=P("guide", "blk"),
        check_vma=False,
    )
```

profile of v0, /device:TPU:0, one launch (start us, length us, event | category | flops | bytes accessed | tf_op | source)
XLA Modules:
  0.0 257.7 jit_solution(10083849745343940406)
XLA Ops:
  6.5 0.0 copy-start
  6.5 0.0 all-reduce.2.cloned.1.call-start
  6.5 1.2 reshape.73
  7.8 1.3 gather_fusion.2
  9.1 1.3 gather_fusion.3
  10.4 0.1 iota_compare_fusion
  10.5 0.7 slice_convert_fusion
  11.2 0.9 fusion.44
  12.1 2.2 fusion.55
  14.3 0.2 fusion.39
  14.5 0.1 copy.17
  14.6 0.0 copy-start.3
  14.6 0.0 copy-start.4
  14.6 0.0 copy-start.6
  14.6 2.4 fusion.4
  17.0 0.0 copy-done.3
  17.0 0.0 copy-start.7
  17.0 0.5 fusion.11
  17.5 45.3 %all_gather.6 = bf16[128,2048]{1,0:T(8,128)(2,1)S(1)} all-gather(bf16[8,2048]{1,0:T(8,128)(2,1)S(1)} %fusion.11), channel_id=1, replica_groups=mesh['guide'=2,'blk'=16] {'blk'}, dimensions={0}, use_global_device_ids=true | all-gather | bytes 557056 | tf_op jit(solution)/shard_map/all_gather | solution.py:79
  62.8 0.0 copy-done.4
  62.8 0.0 copy-done.6
  62.8 0.3 fusion.10
  63.1 38.5 %all_gather.7 = bf16[128,2048]{1,0:T(8,128)(2,1)S(1)} all-gather(bf16[128,128]{1,0:T(8,128)(2,1)S(1)} %fusion.10), channel_id=1, replica_groups=mesh['guide'=2,'blk'=16] {'blk'}, dimensions={1}, use_global_device_ids=true | all-gather | bytes 557056 | tf_op jit(solution)/shard_map/all_gather | solution.py:84
  101.7 0.2 fusion.15
  101.9 0.0 copy-done.7
  101.9 3.5 %fusion.34 = f32[128,684]{0,1:T(8,128)} fusion(bf16[2048,684]{0,1:T(8,128)(2,1)} %param.27, bf16[128,2048]{1,0:T(8,128)(2,1)S(1)} %all_gather.7, f32[2048]{0:T(1024)S(1)} %copy-done.7, f32[128]{0:T(128)S(1)} %add_rsqrt_fusion.1), kind=kOutput, calls=%fused_computation.49 | convolution fusion | flops 359661568 | bytes 3684864 | tf_op jit(solution)/shard_map/dot_general | solution.py:87
  105.4 0.0 copy-done
  105.4 0.0 copy-start.5
  105.4 5.0 %fusion.8 = f32[128,2048]{1,0:T(8,128)} fusion(bf16[684,2048]{1,0:T(8,128)(2,1)S(1)} %copy-done, bf16[2048,684]{0,1:T(8,128)(2,1)} %param.28, f32[128,684]{0,1:T(8,128)} %fusion.34, pred[684]{0:T(1024)(128)(4,1)S(1)} %add_compare_fusion, bf16[128,2048]{1,0:T(8,128)(2,1)S(1)} %all_gather.7, f32[2048]{0:T(1024)S(1)} %copy-done.7, f32[128]{0:T(128)S(1)} %add_rsqrt_fusion.1), kind=kOutput, calls=%fused_computation.21 | convolution fusion | flops 718887424 | bytes 7535788 | tf_op jit(solution)/shard_map/dot_general | solution.py:93
  110.4 0.0 all-reduce.2.cloned.1.call-update
  110.5 109.6 %all-reduce.2.cloned.1.call-done = f32[128,2048]{1,0:T(8,128)} async-done(((f32[128,2048]{1,0:T(8,128)}), f32[128,2048]{1,0:T(8,128)}) %all-reduce.2.cloned.1.call-update) | async-done | bytes 1048592 | tf_op jit(solution)/shard_map/psum | solution.py:94
  220.1 1.4 fusion.12
  221.5 0.0 copy-done.5
  221.5 0.0 copy-start.2
  221.5 0.0 copy-start.1
  221.5 14.7 %fusion.56 = (bf16[128,6400]{1,0:T(8,128)(2,1)}, f32[128,6400]{1,0:T(8,128)}) fusion(bf16[2048,6400]{1,0:T(8,128)(2,1)} %param.31, f32[2048]{0:T(1024)S(1)} %copy-done.5, f32[128]{0:T(128)S(1)} %add_rsqrt_fusion, f32[128,2048]{1,0:T(8,128)} %all-reduce.2.cloned.1.call-done, bf16[128,2048]{1,0:T(8,128)(2,1)S(1)} %all_gather.7), kind=kOutput, calls=%fused_computation.90 | convolution fusion | flops 3358097408 | bytes 32711168 | tf_op jit(solution)/shard_map/dot_general | solution.py:96
  236.2 0.0 collective-permute-start
  236.2 0.0 copy-done.2
  236.2 1.2 scatter_custom_fusion
  237.4 0.0 copy-done.1
  237.4 1.2 gather_fusion
  238.6 0.1 compare_and_fusion
  238.8 1.3 collective-permute-done
  240.1 4.3 %fusion.3 = bf16[128,6400]{1,0:T(8,128)(2,1)} fusion(f32[128,6400]{1,0:T(8,128)} %get-tuple-element.13, bf16[128,6400]{1,0:T(8,128)(2,1)} %collective-permute-done, f32[128]{0:T(128)S(1)} %and_select_fusion.2, pred[]{:T(512)S(6)} %eq.4), kind=kLoop, calls=%fused_computation.10 | loop fusion | flops 5734400 | bytes 6554113 | tf_op jit(solution)/shard_map/convert_element_type | solution.py:109
  244.4 4.3 %gather_fusion.1 = bf16[64,6400]{1,0:T(8,128)(2,1)} fusion(bf16[128,6400]{1,0:T(8,128)(2,1)} %fusion.3, s32[1024]{0:T(1024)S(1)} %pad_clamp_fusion), kind=kCustom, calls=%fused_computation.3 | custom fusion | bytes 1638656 | tf_op jit(solution)/shard_map/jit(_take)/gather | solution.py:112
  248.7 2.2 broadcast_select_fusion
  (15 shorter events, 0.1 us)
Async XLA Ops:
  6.5 98.9 %copy-start = (bf16[684,2048]{1,0:T(8,128)(2,1)S(1)}, bf16[684,2048]{1,0:T(8,128)(2,1)}, u32[]{:S(2)}) copy-start(bf16[684,2048]{1,0:T(8,128)(2,1)} %param.29) | copy-start | bytes 8404996
  6.5 213.5 %all-reduce.2.cloned.1.call-start = ((), (), s32[]{:S(2)}) async-start(), calls=%async_computation | async-start | bytes 2097152 | tf_op jit(solution)/shard_map/psum | solution.py:94
  14.6 2.4 copy-start.3
  14.6 48.3 %copy-start.4 = (bf16[2048,128]{1,0:T(8,128)(2,1)S(1)}, bf16[2048,128]{1,0:T(8,128)(2,1)}, u32[]{:S(2)}) copy-start(bf16[2048,128]{1,0:T(8,128)(2,1)} %param.25) | copy-start | bytes 1572868
  14.6 48.3 %copy-start.6 = (bf16[128,128]{1,0:T(8,128)(2,1)S(1)}, bf16[128,128]{1,0:T(8,128)(2,1)}, u32[]{:S(2)}) copy-start(bf16[128,128]{1,0:T(8,128)(2,1)} %param.17) | copy-start | bytes 98308
  17.0 84.9 %copy-start.7 = (f32[2048]{0:T(1024)S(1)}, f32[2048]{0:T(1024)}, u32[]{:S(2)}) copy-start(f32[2048]{0:T(1024)} %param.26) | copy-start | bytes 24580
  105.4 116.1 %copy-start.5 = (f32[2048]{0:T(1024)S(1)}, f32[2048]{0:T(1024)}, u32[]{:S(2)}) copy-start(f32[2048]{0:T(1024)} %param.30) | copy-start | bytes 24580
  221.5 14.7 %copy-start.2 = (s32[128]{0:T(128)S(1)}, s32[128]{0:T(128)}, u32[]{:S(2)}) copy-start(s32[128]{0:T(128)} %param.22) | copy-start | bytes 1540
  221.5 15.9 %copy-start.1 = (f32[128]{0:T(128)S(1)}, f32[128]{0:T(128)}, u32[]{:S(2)}) copy-start(f32[128]{0:T(128)} %param.23) | copy-start | bytes 1540
  236.2 3.8 %collective-permute-start = (bf16[128,6400]{1,0:T(8,128)(2,1)}, bf16[128,6400]{1,0:T(8,128)(2,1)}, u32[]{:S(2)}, u32[]{:S(2)}) collective-permute-start(bf16[128,6400]{1,0:T(8,128)(2,1)} %get-tuple-element.12), channel_id=1, source_target_pairs={{0,16},{16,0},{1,17},{17,1},{2,18},{18,2},{3,19},{19,3},{4,20},{20... | collective-permute-start | bytes 4915208 | tf_op jit(solution)/shard_map/ppermute | solution.py:12
Sparse Core Ops, SparseCore 0:
  110.6 109.4 all-reduce.1
where the time goes:
time: 258 us
  waiting for transfers between devices  111 us (43%)
  blocking collectives  83.9 us (33%)
  matrix products  29.5 us (11%)
  between operations  13.5 us (5%)
  local copies, waits for them, and re-layouts  10.7 us (4%)
  other arithmetic  9.26 us (4%)
    psum x1, waiting for transfers between devices, body(): summed = lax.psum(partial_sum, 'blk')  110 us
    all_gather x1, blocking collectives, body(): lax.all_gather(value_rows, 'blk', axis=0, tiled=True)  45.3 us
    all_gather x1, blocking collectives, body(): rows_full = lax.all_gather(residual, 'blk', axis=1, tiled=True)  38.5 us
    dot_general x1, matrix products, body(): jnp.dot(rms_round(after_mlp, head_gain), w_head, preferred_element_type=j...  14.7 us
  transfers between devices with their start and end apart: 2, of which 2 were waited for; matrix products, arithmetic and copies ran while one was open for 1% of the time, Pallas kernels for 0%

commit v1 on v0

--- a/solution.py
+++ b/solution.py
@@ -91,7 +91,8 @@
         unit_ids[None, :] < FF, jax.nn.silu(gate_out) * up_out, jnp.float32(0.0)
     ).astype(jnp.bfloat16)
     partial_sum = jnp.dot(hidden, w_down, preferred_element_type=jnp.float32)
-    summed = lax.psum(partial_sum, "blk")
+    parts = lax.all_gather(partial_sum, "blk", axis=0, tiled=False)
+    summed = parts.sum(axis=0)
     after_mlp = (rows_full.astype(jnp.float32) + summed).astype(jnp.bfloat16)
     logits = jnp.dot(rms_round(after_mlp, head_gain), w_head, preferred_element_type=jnp.float32)
     request_count = logits.shape[0]

time: 258 us -> 343 us (1.33)
  waiting for transfers between devices: 111 us -> 190 us
  other arithmetic: 9.26 us -> 15.7 us
    all_gather x0 -> x1, waiting for transfers between devices: none -> 189 us  [body(): parts = lax.all_gather(partial_sum, 'blk', axis=0, tiled=False)]
    psum x1 -> x0, waiting for transfers between devices: 110 us -> none  [body(): summed = lax.psum(partial_sum, 'blk')]
    reduce_sum x0 -> x1, other arithmetic: none -> 7.49 us  [body(): summed = parts.sum(axis=0)]
where the time goes in v1:
time: 343 us
  waiting for transfers between devices  190 us (55%)
  blocking collectives  83.9 us (24%)
  matrix products  28.6 us (8%)
  other arithmetic  15.7 us (5%)
  between operations  13.5 us (4%)
  local copies, waits for them, and re-layouts  10.7 us (3%)
    all_gather x1, waiting for transfers between devices, body(): parts = lax.all_gather(partial_sum, 'blk', axis=0, tiled=False)  189 us
    all_gather x1, blocking collectives, body(): lax.all_gather(value_rows, 'blk', axis=0, tiled=True)  45.3 us
    all_gather x1, blocking collectives, body(): rows_full = lax.all_gather(residual, 'blk', axis=1, tiled=True)  38.5 us
    dot_general x1, matrix products, body(): jnp.dot(rms_round(after_mlp, head_gain), w_head, preferred_element_type=j...  13.8 us
    reduce_sum x1, other arithmetic, body(): summed = parts.sum(axis=0)  7.49 us
  transfers between devices with their start and end apart: 2, of which 2 were waited for; matrix products, arithmetic and copies ran while one was open for 1% of the time, Pallas kernels for 0%

profile of v1, /device:TPU:0, one launch (start us, length us, event | category | flops | bytes accessed | tf_op | source)
XLA Modules:
  0.0 343.0 jit_solution(13303615628374586665)
XLA Ops:
  6.5 0.0 copy-start
  6.5 0.0 all-gather.3.cloned.1.call-start
  6.6 1.4 gather_fusion.2
  8.0 1.3 gather_fusion.3
  9.4 0.1 iota_compare_fusion
  9.4 1.1 reshape.73
  10.5 0.7 slice_convert_fusion
  11.2 0.9 fusion.44
  12.1 2.2 fusion.55
  14.3 0.2 fusion.39
  14.5 0.1 copy.17
  14.6 0.0 copy-start.4
  14.6 0.0 copy-start.5
  14.6 0.0 copy-start.7
  14.6 2.4 fusion.4
  17.0 0.0 copy-done.4
  17.0 0.0 copy-start.8
  17.0 0.5 fusion.11
  17.5 45.3 %all_gather.12 = bf16[128,2048]{1,0:T(8,128)(2,1)S(1)} all-gather(bf16[8,2048]{1,0:T(8,128)(2,1)S(1)} %fusion.11), channel_id=1, replica_groups=mesh['guide'=2,'blk'=16] {'blk'}, dimensions={0}, use_global_device_ids=true | all-gather | bytes 557056 | tf_op jit(solution)/shard_map/all_gather | solution.py:79
  62.8 0.0 copy-done.5
  62.8 0.0 copy-done.7
  62.8 0.3 fusion.10
  63.1 38.5 %all_gather.13 = bf16[128,2048]{1,0:T(8,128)(2,1)S(1)} all-gather(bf16[128,128]{1,0:T(8,128)(2,1)S(1)} %fusion.10), channel_id=1, replica_groups=mesh['guide'=2,'blk'=16] {'blk'}, dimensions={1}, use_global_device_ids=true | all-gather | bytes 557056 | tf_op jit(solution)/shard_map/all_gather | solution.py:84
  101.7 0.2 fusion.15
  101.9 0.0 copy-done.8
  101.9 3.5 %fusion.34 = f32[128,684]{0,1:T(8,128)} fusion(bf16[2048,684]{0,1:T(8,128)(2,1)} %param.27, bf16[128,2048]{1,0:T(8,128)(2,1)S(1)} %all_gather.13, f32[2048]{0:T(1024)S(1)} %copy-done.8, f32[128]{0:T(128)S(1)} %add_rsqrt_fusion.1), kind=kOutput, calls=%fused_computation.49 | convolution fusion | flops 359661568 | bytes 3684864 | tf_op jit(solution)/shard_map/dot_general | solution.py:87
  105.4 0.0 copy-done
  105.4 5.0 %fusion.8 = f32[128,2048]{1,0:T(8,128)} fusion(bf16[684,2048]{1,0:T(8,128)(2,1)S(1)} %copy-done, bf16[2048,684]{0,1:T(8,128)(2,1)} %param.28, f32[128,684]{0,1:T(8,128)} %fusion.34, pred[684]{0:T(1024)(128)(4,1)S(1)} %add_compare_fusion, bf16[128,2048]{1,0:T(8,128)(2,1)S(1)} %all_gather.13, f32[2048]{0:T(1024)S(1)} %copy-done.8, f32[128]{0:T(128)S(1)} %add_rsqrt_fusion.1), kind=kOutput, calls=%fused_computation.21 | convolution fusion | flops 718887424 | bytes 7535788 | tf_op jit(solution)/shard_map/dot_general | solution.py:93
  110.4 0.0 all-gather.3.cloned.1.call-update
  110.5 189.4 %all-gather.3.cloned.1.call-done = f32[2048,2048]{1,0:T(8,128)} async-done(((f32[128,2048]{1,0:T(8,128)}), f32[2048,2048]{1,0:T(8,128)}) %all-gather.3.cloned.1.call-update) | async-done | bytes 16777232 | tf_op jit(solution)/shard_map/all_gather | solution.py:94
  299.8 0.0 copy-start.6
  299.8 7.5 %reduce_sum.38 = f32[128,2048]{1,0:T(8,128)S(1)} reduce(f32[16,128,2048]{2,1,0:T(8,128)} %bitcast.24, f32[]{:T(128)} %constant.46.clone.1), dimensions={0}, to_apply=%region_4.6 | reduce | flops 3932160 | bytes 17825796 | tf_op jit(solution)/shard_map/reduce_sum | solution.py:95
  307.3 0.2 fusion.12
  307.6 0.0 copy-done.6
  307.6 0.0 copy-start.3
  307.6 0.0 copy-start.2
  307.6 13.8 %fusion.56 = (bf16[128,6400]{1,0:T(8,128)(2,1)S(1)}, f32[128,6400]{1,0:T(8,128)}) fusion(bf16[2048,6400]{1,0:T(8,128)(2,1)} %param.31, f32[2048]{0:T(1024)S(1)} %copy-done.6, f32[128]{0:T(128)S(1)} %add_rsqrt_fusion, f32[128,2048]{1,0:T(8,128)S(1)} %reduce_sum.38, bf16[128,2048]{1,0:T(8,128)(2,1)S(1)} %all_gather.13), kind=kOutput, calls=%fused_computation.90 | convolution fusion | flops 3358097408 | bytes 32711168 | tf_op jit(solution)/shard_map/dot_general | solution.py:97
  321.4 0.0 collective-permute-start
  321.4 0.0 copy-done.3
  321.5 1.2 scatter_custom_fusion
  322.6 0.0 copy-done.2
  322.7 1.2 gather_fusion
  323.9 0.1 compare_and_fusion
  324.0 1.1 collective-permute-done
  325.1 0.0 copy-start.1
  325.1 4.5 %fusion.3 = bf16[128,6400]{1,0:T(8,128)(2,1)} fusion(f32[128,6400]{1,0:T(8,128)} %get-tuple-element.13, bf16[128,6400]{1,0:T(8,128)(2,1)} %collective-permute-done, f32[128]{0:T(128)S(1)} %and_select_fusion.2, pred[]{:T(512)S(6)} %eq.4), kind=kLoop, calls=%fused_computation.10 | loop fusion | flops 5734400 | bytes 6554113 | tf_op jit(solution)/shard_map/convert_element_type | solution.py:110
  329.6 4.3 %gather_fusion.1 = bf16[64,6400]{1,0:T(8,128)(2,1)} fusion(bf16[128,6400]{1,0:T(8,128)(2,1)} %fusion.3, s32[1024]{0:T(1024)S(1)} %pad_clamp_fusion), kind=kCustom, calls=%fused_computation.3 | custom fusion | bytes 1638656 | tf_op jit(solution)/shard_map/jit(_take)/gather | solution.py:113
  333.9 2.2 broadcast_select_fusion
  336.1 0.0 copy-done.1
  (15 shorter events, 0.1 us)
Async XLA Ops:
  6.5 98.9 %copy-start = (bf16[684,2048]{1,0:T(8,128)(2,1)S(1)}, bf16[684,2048]{1,0:T(8,128)(2,1)}, u32[]{:S(2)}) copy-start(bf16[684,2048]{1,0:T(8,128)(2,1)} %param.29) | copy-start | bytes 8404996
  6.5 293.3 %all-gather.3.cloned.1.call-start = ((), (), s32[]{:S(2)}) async-start(), calls=%async_computation | async-start | bytes 17825792 | tf_op jit(solution)/shard_map/all_gather | solution.py:94
  14.6 2.4 copy-start.4
  14.6 48.3 %copy-start.5 = (bf16[2048,128]{1,0:T(8,128)(2,1)S(1)}, bf16[2048,128]{1,0:T(8,128)(2,1)}, u32[]{:S(2)}) copy-start(bf16[2048,128]{1,0:T(8,128)(2,1)} %param.25) | copy-start | bytes 1572868
  14.6 48.3 %copy-start.7 = (bf16[128,128]{1,0:T(8,128)(2,1)S(1)}, bf16[128,128]{1,0:T(8,128)(2,1)}, u32[]{:S(2)}) copy-start(bf16[128,128]{1,0:T(8,128)(2,1)} %param.17) | copy-start | bytes 98308
  17.0 84.9 %copy-start.8 = (f32[2048]{0:T(1024)S(1)}, f32[2048]{0:T(1024)}, u32[]{:S(2)}) copy-start(f32[2048]{0:T(1024)} %param.26) | copy-start | bytes 24580
  299.8 7.7 %copy-start.6 = (f32[2048]{0:T(1024)S(1)}, f32[2048]{0:T(1024)}, u32[]{:S(2)}) copy-start(f32[2048]{0:T(1024)} %param.30) | copy-start | bytes 24580
  307.6 13.9 %copy-start.3 = (s32[128]{0:T(128)S(1)}, s32[128]{0:T(128)}, u32[]{:S(2)}) copy-start(s32[128]{0:T(128)} %param.22) | copy-start | bytes 1540
  307.6 15.1 %copy-start.2 = (f32[128]{0:T(128)S(1)}, f32[128]{0:T(128)}, u32[]{:S(2)}) copy-start(f32[128]{0:T(128)} %param.23) | copy-start | bytes 1540
  321.4 3.6 %collective-permute-start = (bf16[128,6400]{1,0:T(8,128)(2,1)S(1)}, bf16[128,6400]{1,0:T(8,128)(2,1)}, u32[]{:S(2)}, u32[]{:S(2)}) collective-permute-start(bf16[128,6400]{1,0:T(8,128)(2,1)S(1)} %get-tuple-element.12), channel_id=1, source_target_pairs={{0,16},{16,0},{1,17},{17,1},{2,18},{18,2},{3,19},{19,3},{4,20},{20... | collective-permute-start | bytes 4915208 | tf_op jit(solution)/shard_map/ppermute | solution.py:12
  325.1 11.0 %copy-start.1 = (bf16[684,2048]{1,0:T(8,128)(2,1)S(1)}, bf16[684,2048]{1,0:T(8,128)(2,1)}, u32[]{:S(2)}) copy-start(bf16[684,2048]{1,0:T(8,128)(2,1)} %param.29) | copy-start | bytes 8404996
Sparse Core Ops, SparseCore 0:
  110.6 189.2 all-gather.2
